TPU v7x, 128 devices: a whole 4x4x4 slice. The times are simulated.
128 devices in a mesh: dp: 4 (over z_hi, core), expert: 32 (over z_lo, y, x).
Axes of the slice: x: 4, y: 4, z: 4 (z_hi: 2, z_lo: 2; z = z_hi * 2 + z_lo), core: 2. Of those that a mesh axis runs over, the one named last changes fastest.
Arguments:
- queries: bfloat16 [1024, 4096], P(('dp', 'expert')), may hold values from -9 to 9
- kv_pool: bfloat16 [16384, 16, 1024], P(('dp', 'expert')), may hold values from -9 to 9
- page_table: int32 [1024, 4, 16], P(('dp', 'expert')), may hold values from 0 to 127
- held_tokens: int32 [1024, 4], P(('dp', 'expert')), may hold values from 1 to 256, as said below
- sinks: float32 [64], replicated, may hold values from 2 to 8
- residual: bfloat16 [1024, 2880], P(('dp', 'expert')), may hold values from -100 to 100
- route_ids: int32 [1024, 4], P(('dp', 'expert')), may hold values from 0 to 31, all different within a row; in each aligned block of 8 rows (0 to 7, 8 to 15, ...) at most 2 rows name the same one
- route_weights: float32 [1024, 4], P(('dp', 'expert')), may hold values from 0.1 to 1
- moe_gain: float32 [2880], replicated, may hold values from 0.25 to 1.75
- w_gate: bfloat16 [32, 2880, 1536], P('expert', None, 'dp')
- w_up: bfloat16 [32, 2880, 1536], P('expert', None, 'dp')
- w_down: bfloat16 [32, 1536, 2880], P('expert', 'dp'), may hold values from -0.078125 to 0.078125
- o_weight: bfloat16 [4096, 2880], P(None, 'dp'), may hold values from -0.09375 to 0.09375
- attn_gain: float32 [2880], replicated, may hold values from 0.25 to 1.75
- qkv_weight: bfloat16 [2880, 5120], P(None, 'dp'), may hold values from -0.109375 to 0.109375
Outputs:
- next_stream: bfloat16 [1024, 2880], P(('dp', 'expert'))
- next_qkv: bfloat16 [1024, 5120], P(('dp', 'expert'))
Inputs may be any that keep to these rules, and one draw needn't show every extreme that they name: `route_ids`: each row names 4 different experts; among the 8 rows of one device no expert is named more than 2 times, a bound that some block reaches. `page_table`: pages may be shared between requests. `held_tokens`: the largest value is reached in every draw.
All inputs are finite; a program needn't handle non-finite values.
Results may differ from a plain program's by a relative error of at most 0.0145.
Values may be sent and summed in bfloat16 or wider, within the bound.
A program may use at most 128 MiB of HBM per device.

v0:
```python
import math
import jax
import jax.numpy as jnp
from jax import lax
from jax.sharding import PartitionSpec as P

HEADS = 64
KVH = 8
HD = 64
TOP = 4
PAGE = 16
PPH = 16
EPSILON = 1e-05
LIMIT = 7.0


def rms_scale(values, gain):
    wide = values.astype(jnp.float32)
    scale = lax.rsqrt(jnp.mean(wide * wide, axis=-1, keepdims=True) + EPSILON)
    return (wide * scale * gain).astype(jnp.bfloat16)


def scale_heads(numerator, factor):
    return numerator * jnp.repeat(factor, HD, axis=1)


def head_tables():
    groups = HEADS // KVH
    columns = jnp.arange(KVH * HD, dtype=jnp.int32)
    head_group = jnp.arange(HEADS, dtype=jnp.int32) // groups
    head_mask = columns[None, :] // HD == head_group[:, None]
    fold_table = (columns[:, None] % HD == jnp.arange(HD, dtype=jnp.int32)[None, :]).astype(
        jnp.float32
    )
    return (head_mask, fold_table)


def holder_block(query_rows, page_rows, count_rows, kv_pool, head_mask, fold_table):
    blocks = query_rows.shape[0]
    token_span = PPH * PAGE
    width = KVH * HD
    fetched = kv_pool[page_rows].reshape(blocks, token_span, 2 * width)
    keys_part = fetched[:, :, :width]
    values_part = fetched[:, :, width:]
    query_heads = query_rows.reshape(blocks, HEADS, HD)
    spread = jnp.where(
        head_mask[None], jnp.tile(query_heads, (1, 1, KVH)), jnp.zeros((), jnp.bfloat16)
    )
    scores = jnp.einsum("bhe,ble->bhl", spread, keys_part, preferred_element_type=jnp.float32) * (
        1.0 / math.sqrt(HD)
    )
    usable = (jnp.arange(token_span, dtype=jnp.int32)[None, :] < count_rows[:, None])[:, None, :]
    highest = jnp.max(jnp.where(usable, scores, -1e30), axis=-1)
    weights = jnp.where(usable, jnp.exp(scores - highest[..., None]), 0.0)
    totals = jnp.sum(weights, axis=-1)
    every_value = jnp.einsum(
        "bhl,ble->bhe",
        weights.astype(jnp.bfloat16),
        values_part,
        preferred_element_type=jnp.float32,
    )
    own_value = jnp.where(head_mask[None], every_value, 0.0)
    numerator = jnp.einsum("bhe,ed->bhd", own_value, fold_table, precision=lax.Precision.HIGHEST)
    return (highest, totals, numerator.reshape(blocks, HEADS * HD))


def expert_apply(rows, gate_w, up_w, down_w):
    gate_proj = jnp.minimum(jnp.dot(rows, gate_w, preferred_element_type=jnp.float32), LIMIT)
    up_proj = jnp.clip(jnp.dot(rows, up_w, preferred_element_type=jnp.float32), -LIMIT, LIMIT)
    activated = (gate_proj * jax.nn.sigmoid(1.702 * gate_proj) * (up_proj + 1.0)).astype(
        jnp.bfloat16
    )
    return jnp.dot(activated, down_w, preferred_element_type=jnp.float32)


def body(
    queries,
    kv_pool,
    page_table,
    held_tokens,
    sinks,
    residual,
    route_ids,
    route_weights,
    moe_gain,
    w_gate,
    w_up,
    w_down,
    o_weight,
    attn_gain,
    qkv_weight,
):
    dp_count = lax.axis_size("dp")
    experts_count = lax.axis_size("expert")
    own_rows = queries.shape[0]
    tables, held_rows = (
        lax.all_gather(page_table, "dp", axis=0, tiled=True),
        lax.all_gather(held_tokens, "dp", axis=0, tiled=True),
    )
    group_queries = lax.all_gather(queries, "dp", axis=0, tiled=True)
    holder = lax.axis_index("dp")
    own_pages = lax.dynamic_index_in_dim(tables, holder, 1, keepdims=False)
    own_counts = lax.dynamic_index_in_dim(held_rows, holder, 1, keepdims=False)
    group_rows = group_queries.shape[0]
    block_rows = 32
    step_total = group_rows // block_rows
    head_mask, fold_table = head_tables()

    def run_block(items):
        return holder_block(items[0], items[1], items[2], kv_pool, head_mask, fold_table)

    highest, totals, numerator = lax.map(
        run_block,
        (
            group_queries.reshape(step_total, block_rows, HEADS * HD),
            own_pages.reshape(step_total, block_rows, PPH),
            own_counts.reshape(step_total, block_rows),
        ),
    )
    highest = highest.reshape(group_rows, HEADS)
    totals = totals.reshape(group_rows, HEADS)
    numerator = numerator.reshape(group_rows, HEADS * HD)
    peak_score = lax.pmax(highest, "dp")
    factor = jnp.exp(highest - peak_score)
    totals, numerator = (
        lax.psum((totals * factor).astype(jnp.bfloat16), "dp").astype(jnp.float32),
        lax.psum(scale_heads(numerator, factor).astype(jnp.bfloat16), "dp").astype(jnp.float32),
    )
    highest = peak_score
    ceiling = jnp.maximum(highest, sinks[None, :])
    kept = jnp.exp(highest - ceiling)
    denominator = totals * kept + jnp.exp(sinks[None, :] - ceiling)
    attention = scale_heads(numerator, kept / denominator).astype(jnp.bfloat16)
    projected = jnp.dot(attention, o_weight, preferred_element_type=jnp.float32).astype(
        jnp.bfloat16
    )
    attention_out = lax.all_to_all(projected, "dp", split_axis=0, concat_axis=1, tiled=True)
    stream = (residual.astype(jnp.float32) + attention_out.astype(jnp.float32)).astype(jnp.bfloat16)
    moe_input = rms_scale(stream, moe_gain)
    capacity = 2 * own_rows * TOP // experts_count
    chosen = (
        route_ids[:, :, None] == jnp.arange(experts_count, dtype=jnp.int32)[None, None, :]
    ).astype(jnp.int32)
    flat_chosen = chosen.reshape(own_rows * TOP, experts_count)
    before = jnp.cumsum(flat_chosen, axis=0) - flat_chosen
    slot_index = jnp.sum(before * flat_chosen, axis=1).reshape(own_rows, TOP)
    placed = chosen[:, :, :, None] * (
        slot_index[:, :, None, None] == jnp.arange(capacity, dtype=jnp.int32)[None, None, None, :]
    ).astype(jnp.int32)
    placed = placed.reshape(own_rows, TOP, experts_count * capacity)
    dispatch = jnp.sum(placed, axis=1).astype(jnp.bfloat16)
    route_share = route_weights / jnp.sum(route_weights, axis=1, keepdims=True)
    combine = jnp.einsum(
        "rk,rkc->rc", route_share, placed.astype(jnp.float32), precision=lax.Precision.HIGHEST
    )
    send_rows = jnp.einsum(
        "rc,rd->cd", dispatch, moe_input, preferred_element_type=jnp.float32
    ).astype(jnp.bfloat16)
    gate_local = w_gate[0]
    up_local = w_up[0]
    down_local = w_down[0]
    copies = jnp.broadcast_to(send_rows[None], (dp_count,) + send_rows.shape).reshape(
        dp_count * send_rows.shape[0], send_rows.shape[1]
    )
    arrived = lax.all_to_all(copies, ("dp", "expert"), split_axis=0, concat_axis=0, tiled=True)
    partial_value = expert_apply(arrived, gate_local, up_local, down_local)
    came_back = lax.all_to_all(
        partial_value.astype(jnp.bfloat16),
        ("dp", "expert"),
        split_axis=0,
        concat_axis=0,
        tiled=True,
    ).astype(partial_value.dtype)
    returned = jnp.sum(came_back.reshape(dp_count, send_rows.shape[0], send_rows.shape[1]), axis=0)
    moe_out = jnp.dot(
        combine, returned, precision=lax.Precision.HIGHEST, preferred_element_type=jnp.float32
    )
    next_stream = (stream.astype(jnp.float32) + moe_out).astype(jnp.bfloat16)
    qkv_input = rms_scale(next_stream, attn_gain)
    group_qkv = jnp.dot(
        lax.all_gather(qkv_input, "dp", axis=0, tiled=True),
        qkv_weight,
        preferred_element_type=jnp.float32,
    ).astype(jnp.bfloat16)
    next_qkv = lax.all_to_all(group_qkv, "dp", split_axis=0, concat_axis=1, tiled=True)
    return (next_stream, next_qkv)


def solution(mesh):
    in_specs = (
        P(("dp", "expert"), None),
        P(("dp", "expert"), None, None),
        P(("dp", "expert"), None, None),
        P(("dp", "expert"), None),
        P(),
        P(("dp", "expert"), None),
        P(("dp", "expert"), None),
        P(("dp", "expert"), None),
        P(),
        P("expert", None, "dp"),
        P("expert", None, "dp"),
        P("expert", "dp", None),
        P(None, "dp"),
        P(),
        P(None, "dp"),
    )
    out_specs = (P(("dp", "expert"), None), P(("dp", "expert"), None))
    return jax.shard_map(body, mesh=mesh, in_specs=in_specs, out_specs=out_specs, check_vma=False)
```

profile of v0, /device:TPU:1, one launch (start us, length us, event | category | flops | bytes accessed | tf_op | source)
XLA Modules:
  0.0 265.4 jit_solution(2009156426341383861)
XLA Ops:
  7.2 0.0 copy-start
  7.2 0.0 all-reduce.2.cloned.1.call-start
  7.3 8.6 %all-gather = s32[4,8,4]{1,2,0:T(4,128)S(1)} all-gather(s32[1,8,4]{1,2,0:T(4,128)} %bitcast.60), channel_id=1, replica_groups=mesh['dp'=4,'expert'=32] {'dp'}, dimensions={0}, use_global_device_ids=true | all-gather | bytes 640 | tf_op jit(solution)/shard_map/all_gather | solution.py:98
  15.9 0.1 reshape.257
  16.0 0.1 iota_compare_fusion.2
  16.1 7.2 %all_gather.14 = s32[32,4,16]{2,1,0:T(4,128)S(1)} all-gather(s32[8,4,16]{2,1,0:T(4,128)} %param.17), channel_id=1, replica_groups=mesh['dp'=4,'expert'=32] {'dp'}, dimensions={0}, use_global_device_ids=true | all-gather | bytes 10240 | tf_op jit(solution)/shard_map/all_gather | solution.py:97
  23.3 0.1 reshape.248
  23.4 7.7 %all_gather.13 = bf16[32,4096]{1,0:T(8,128)(2,1)S(1)} all-gather(bf16[8,4096]{1,0:T(8,128)(2,1)} %param.15), channel_id=1, replica_groups=mesh['dp'=4,'expert'=32] {'dp'}, dimensions={0}, use_global_device_ids=true | all-gather | bytes 327680 | tf_op jit(solution)/shard_map/all_gather | solution.py:100
  31.1 0.5 tile.14
  31.7 2.7 %tile.15 = bf16[32,64,8,64]{3,2,1,0:T(8,128)(2,1)} broadcast(bf16[32,64,64]{2,1,0:T(8,128)(2,1)S(1)} %tile.14), dimensions={0,1,3} | broadcast | bytes 2359296 | tf_op jit(solution)/shard_map/while/body/eval_jaxpr/tile | solution.py:47
  34.4 6.4 %tile.16 = bf16[32,64,512]{2,1,0:T(8,128)(2,1)} reshape(bf16[32,64,8,64]{3,2,1,0:T(8,128)(2,1)} %tile.15) | data formatting | bytes 4194304 | tf_op jit(solution)/shard_map/while/body/eval_jaxpr/tile | solution.py:47
  40.8 16.1 %gather_fusion = bf16[512,16,1024]{2,1,0:T(8,128)(2,1)} fusion(bf16[128,16,1024]{2,1,0:T(8,128)(2,1)} %param.16, s32[1024]{0:T(1024)S(1)} %pad_clamp_fusion), kind=kCustom, calls=%fused_computation | custom fusion | bytes 33556480 | tf_op jit(solution)/shard_map/while/body/eval_jaxpr/gather | solution.py:42
  56.9 0.1 broadcast_compare_fusion
  57.0 8.0 %select_reduce_fusion = (f32[32,64]{1,0:T(8,128)S(1)}, f32[32,64,256]{2,1,0:T(8,128)}) fusion(pred[32,256]{1,0:T(8,128)(4,1)S(1)} %iota_compare_fusion.2, bf16[32,256,1024]{2,1,0:T(8,128)(2,1)} %bitcast.54, bf16[32,64,512]{2,1,0:T(8,128)(2,1)} %tile.16, pred[64,512]{1,0:T(8,128)(4,1)S(1)} %broadcast_compare_fusion), kind=kOutput, calls=%fused_computation.20 | convolution fusion | flops 539490304 | bytes 12632064 | tf_op jit(solution)/shard_map/while/body/eval_jaxpr/bhe,ble->bhl/dot_general | solution.py:49
  65.1 12.4 %pmax.7 = f32[32,64]{1,0:T(8,128)S(1)} all-reduce(f32[32,64]{1,0:T(8,128)S(1)} %get-tuple-element.28), channel_id=1, replica_groups=mesh['dp'=4,'expert'=32] {'dp'}, use_global_device_ids=true, to_apply=%region_1.2 | all-reduce | flops 2048 | bytes 16384 | tf_op jit(solution)/shard_map/pmax | solution.py:123
  77.5 2.5 fusion.17
  80.0 0.0 copy-done.1
  80.0 4.3 %fusion = f32[32,64,512]{2,1,0:T(8,128)S(1)} fusion(bf16[32,256,1024]{2,1,0:T(8,128)(2,1)} %bitcast.55, f32[32,64,256]{2,1,0:T(8,128)S(1)} %copy-done.1, f32[32,64]{1,0:T(8,128)S(1)} %get-tuple-element.28, pred[32,256]{1,0:T(8,128)(4,1)S(1)} %iota_compare_fusion.2), kind=kOutput, calls=%fused_computation.1 | convolution fusion | flops 538968064 | bytes 14696448 | tf_op jit(solution)/shard_map/while/body/eval_jaxpr/bhl,ble->bhe/dot_general | solution.py:56
  84.4 0.0 copy-start.6
  84.4 0.0 copy-start.8
  84.4 2.2 fusion.22
  86.6 1.2 convert_element_type.109
  87.8 0.0 all-reduce.2.cloned.1.call-update
  87.8 10.5 %psum.15 = bf16[32,64]{1,0:T(8,128)(2,1)S(1)} all-reduce(bf16[32,64]{1,0:T(8,128)(2,1)S(1)} %get-tuple-element.24), channel_id=1, replica_groups=mesh['dp'=4,'expert'=32] {'dp'}, use_global_device_ids=true, to_apply=%region_4.5 | all-reduce | flops 2048 | bytes 8192 | tf_op jit(solution)/shard_map/psum | solution.py:126
  98.4 0.0 copy-done.6
  98.4 0.1 copy.28
  98.4 0.1 eq.93
  98.5 0.1 fusion.76
  98.6 0.1 reduce_window_sum.11
  98.7 0.2 select_reduce_fusion.1
  98.8 0.1 eq.97
  98.9 0.1 copy.29
  99.1 0.3 broadcast_in_dim.108
  99.4 1.2 reshape.243
  100.6 0.0 copy-start.3
  100.6 0.0 copy-start.5
  100.6 30.9 %all-reduce.2.cloned.1.call-done = bf16[32,4096]{1,0:T(8,128)(2,1)} async-done(((bf16[32,4096]{1,0:T(8,128)(2,1)}), bf16[32,4096]{1,0:T(8,128)(2,1)}) %all-reduce.2.cloned.1.call-update) | async-done | bytes 262160 | tf_op jit(solution)/shard_map/psum | solution.py:127
  131.5 5.3 %fusion.40 = bf16[4,8,720]{2,1,0:T(8,128)(2,1)} fusion(bf16[4096,720]{0,1:T(8,128)(2,1)} %param.27, f32[32,4096]{1,0:T(8,128)} %reshape.243, bf16[32,4096]{1,0:T(8,128)(2,1)} %all-reduce.2.cloned.1.call-done), kind=kOutput, calls=%fused_computation.34 | convolution fusion | flops 189159936 | bytes 6730752 | tf_op jit(solution)/shard_map/dot_general | solution.py:134
  136.9 3.4 %all-to-all-start = ((bf16[4,8,720]{2,1,0:T(8,128)(2,1)}), bf16[4,8,720]{2,1,0:T(8,128)(2,1)S(1)}, u32[]{:S(2)}, u32[]{:S(2)}) async-start(bf16[4,8,720]{2,1,0:T(8,128)(2,1)} %fusion.40), calls=%async_computation | async-start | bytes 98304 | tf_op jit(solution)/shard_map/all_to_all | solution.py:137
  140.3 0.1 multiply_reduce_fusion
  140.4 4.6 %all-to-all-done = bf16[4,8,720]{2,1,0:T(8,128)(2,1)S(1)} async-done(((bf16[4,8,720]{2,1,0:T(8,128)(2,1)}), bf16[4,8,720]{2,1,0:T(8,128)(2,1)S(1)}, u32[]{:S(2)}, u32[]{:S(2)}) %all-to-all-start) | async-done | bytes 46112 | tf_op jit(solution)/shard_map/all_to_all | solution.py:137
  145.1 0.1 reshape.244
  145.2 0.1 fusion.64
  145.3 0.3 convolution_convert_fusion.1
  145.7 1.2 broadcast_in_dim.109
  146.9 4.3 %all_to_all.40 = bf16[128,2,2880]{2,1,0:T(2,128)(2,1)} reshape(bf16[4,64,2880]{2,1,0:T(8,128)(2,1)} %broadcast_in_dim.109) | data formatting | bytes 2949120 | tf_op jit(solution)/shard_map/all_to_all | solution.py:165
  151.2 30.7 %all_to_all.53 = bf16[128,2,2880]{2,1,0:T(2,128)(2,1)} all-to-all(bf16[128,2,2880]{2,1,0:T(2,128)(2,1)} %all_to_all.40), channel_id=1, replica_groups=mesh['dp'=4,'expert'=32] {'dp','expert'}, dimensions={0} | all-to-all | bytes 2949120 | tf_op jit(solution)/shard_map/all_to_all | solution.py:165
  181.9 4.4 %all_to_all.42 = bf16[256,2880]{1,0:T(8,128)(2,1)} reshape(bf16[128,2,2880]{2,1,0:T(2,128)(2,1)} %all_to_all.53) | data formatting | bytes 2949120 | tf_op jit(solution)/shard_map/all_to_all | solution.py:165
  186.3 3.0 %fusion.25 = f32[256,384]{1,0:T(8,128)S(1)} fusion(bf16[256,2880]{1,0:T(8,128)(2,1)} %all_to_all.42, bf16[1,2880,384]{2,1,0:T(8,128)(2,1)} %param.24), kind=kOutput, calls=%fused_computation.28 | convolution fusion | flops 566329344 | bytes 4079616 | tf_op jit(solution)/shard_map/dot_general | solution.py:68
  189.3 5.1 %convolution_convert_fusion = bf16[256,2880]{0,1:T(8,128)(2,1)} fusion(bf16[1,384,2880]{1,2,0:T(8,128)(2,1)S(1)} %copy-done, bf16[256,2880]{1,0:T(8,128)(2,1)} %all_to_all.42, bf16[1,2880,384]{2,1,0:T(8,128)(2,1)} %param.25, f32[256,384]{1,0:T(8,128)S(1)} %fusion.25), kind=kOutput, calls=%fused_computation.7 | convolution fusion | flops 1134084096 | bytes 7766016 | tf_op jit(solution)/shard_map/dot_general | solution.py:73
  194.4 2.6 copy.30
  197.0 4.3 %all_to_all.43 = bf16[128,2,2880]{2,1,0:T(2,128)(2,1)} reshape(bf16[256,2880]{1,0:T(8,128)(2,1)} %copy.30) | data formatting | bytes 2949120 | tf_op jit(solution)/shard_map/all_to_all | solution.py:167
  201.3 6.1 %all-to-all-start.2 = ((bf16[128,2,2880]{2,1,0:T(2,128)(2,1)}), bf16[128,2,2880]{2,1,0:T(2,128)(2,1)}, u32[]{:S(2)}, u32[]{:S(2)}) async-start(bf16[128,2,2880]{2,1,0:T(2,128)(2,1)} %all_to_all.43), calls=%async_computation.2 | async-start | bytes 3014656 | tf_op jit(solution)/shard_map/all_to_all | solution.py:167
  207.4 23.1 %all-to-all-done.2 = bf16[128,2,2880]{2,1,0:T(2,128)(2,1)} async-done(((bf16[128,2,2880]{2,1,0:T(2,128)(2,1)}), bf16[128,2,2880]{2,1,0:T(2,128)(2,1)}, u32[]{:S(2)}, u32[]{:S(2)}) %all-to-all-start.2) | async-done | bytes 1474592 | tf_op jit(solution)/shard_map/all_to_all | solution.py:167
  230.5 4.5 %reshape.245 = f32[4,64,2880]{2,1,0:T(8,128)} reshape(bf16[128,2,2880]{2,1,0:T(2,128)(2,1)} %all-to-all-done.2) | data formatting | bytes 4423680 | tf_op jit(solution)/shard_map/convert_element_type | solution.py:173
  235.1 2.1 reduce_sum.69
  237.2 0.6 fusion.61
  237.8 0.0 copy-start.2
  237.8 0.1 fusion.63
  237.9 8.4 %all_gather.15 = bf16[32,2880]{1,0:T(8,128)(2,1)S(1)} all-gather(bf16[8,2880]{1,0:T(8,128)(2,1)S(1)} %fusion.63), channel_id=1, replica_groups=mesh['dp'=4,'expert'=32] {'dp'}, dimensions={0}, use_global_device_ids=true | all-gather | bytes 230400 | tf_op jit(solution)/shard_map/all_gather | solution.py:181
  246.3 4.3 %fusion.7 = bf16[4,8,1280]{2,1,0:T(8,128)(2,1)S(1)} fusion(bf16[32,2880]{1,0:T(8,128)(2,1)S(1)} %all_gather.15, bf16[2880,1280]{1,0:T(8,128)(2,1)} %param.29), kind=kOutput, calls=%fused_computation.12 | convolution fusion | flops 235970560 | bytes 7639040 | tf_op jit(solution)/shard_map/dot_general | solution.py:180
  250.6 0.0 copy-done.2
  250.6 7.3 %all_to_all.54 = bf16[4,8,1280]{2,1,0:T(8,128)(2,1)S(1)} all-to-all(bf16[4,8,1280]{2,1,0:T(8,128)(2,1)S(1)} %fusion.7), channel_id=1, replica_groups=mesh['dp'=4,'expert'=32] {'dp'}, dimensions={0} | all-to-all | bytes 163840 | tf_op jit(solution)/shard_map/all_to_all | solution.py:185
  257.9 0.6 copy.40
  (29 shorter events, 0.3 us)
Async XLA Ops:
  7.2 182.2 %copy-start = (bf16[1,384,2880]{1,2,0:T(8,128)(2,1)S(1)}, bf16[1,384,2880]{1,2,0:T(8,128)(2,1)}, u32[]{:S(2)}) copy-start(bf16[1,384,2880]{1,2,0:T(8,128)(2,1)} %param.26) | copy-start | bytes 6635524
  7.2 124.3 %all-reduce.2.cloned.1.call-start = ((), (), s32[]{:S(2)}) async-start(), calls=%async_computation.4 | async-start | bytes 524288 | tf_op jit(solution)/shard_map/psum | solution.py:127
  77.5 2.5 copy-start.1
  84.4 14.0 %copy-start.6 = (s32[8,4]{0,1:T(4,128)S(1)}, s32[8,4]{0,1:T(4,128)}, u32[]{:S(2)}) copy-start(s32[8,4]{0,1:T(4,128)} %param.21) | copy-start | bytes 388
  84.4 14.6 %copy-start.8 = (f32[64]{0:T(128)S(1)}, f32[64]{0:T(128)}, u32[]{:S(2)}) copy-start(f32[64]{0:T(128)} %param.19) | copy-start | bytes 772
  100.6 44.6 %copy-start.3 = (bf16[8,2880]{1,0:T(8,128)(2,1)S(1)}, bf16[8,2880]{1,0:T(8,128)(2,1)}, u32[]{:S(2)}) copy-start(bf16[8,2880]{1,0:T(8,128)(2,1)} %param.20) | copy-start | bytes 138244
  100.6 44.8 %copy-start.5 = (f32[2880]{0:T(1024)S(1)}, f32[2880]{0:T(1024)}, u32[]{:S(2)}) copy-start(f32[2880]{0:T(1024)} %param.23) | copy-start | bytes 34564
  136.9 8.1 %all-to-all-start = ((bf16[4,8,720]{2,1,0:T(8,128)(2,1)}), bf16[4,8,720]{2,1,0:T(8,128)(2,1)S(1)}, u32[]{:S(2)}, u32[]{:S(2)}) async-start(bf16[4,8,720]{2,1,0:T(8,128)(2,1)} %fusion.40), calls=%async_computation | async-start | bytes 98304 | tf_op jit(solution)/shard_map/all_to_all | solution.py:137
  201.3 6.1 %copy-start.7 = (f32[8,4]{0,1:T(4,128)S(1)}, f32[8,4]{0,1:T(4,128)}, u32[]{:S(2)}) copy-start(f32[8,4]{0,1:T(4,128)} %param.22) | copy-start | bytes 388
  201.3 29.3 %all-to-all-start.2 = ((bf16[128,2,2880]{2,1,0:T(2,128)(2,1)}), bf16[128,2,2880]{2,1,0:T(2,128)(2,1)}, u32[]{:S(2)}, u32[]{:S(2)}) async-start(bf16[128,2,2880]{2,1,0:T(2,128)(2,1)} %all_to_all.43), calls=%async_computation.2 | async-start | bytes 3014656 | tf_op jit(solution)/shard_map/all_to_all | solution.py:167
  235.0 2.7 %copy-start.4 = (f32[2880]{0:T(1024)S(1)}, f32[2880]{0:T(1024)}, u32[]{:S(2)}) copy-start(f32[2880]{0:T(1024)} %param.28) | copy-start | bytes 34564
  237.8 12.8 %copy-start.2 = (bf16[8,2880]{1,0:T(8,128)(2,1)}, bf16[8,2880]{1,0:T(8,128)(2,1)S(1)}, u32[]{:S(2)}) copy-start(bf16[8,2880]{1,0:T(8,128)(2,1)S(1)} %get-tuple-element.44) | copy-start | bytes 138244
Sparse Core Ops, SparseCore 0:
  87.9 43.5 all-reduce.1
where the time goes:
time: 266 us; the launch traced here: 265 us
  blocking collectives  93 us (35%)
  waiting for transfers between devices  58.7 us (22%)
  local copies, waits for them, and re-layouts  51.1 us (19%)
  matrix products  33.2 us (12%)
  between operations  14.3 us (5%)
  starting transfers between devices  9.51 us (4%)
  other arithmetic  5.52 us (2%)
    psum x1, waiting for transfers between devices, body(): lax.psum(scale_heads(numerator, factor).astype(jnp.bfloat16), 'dp')  30.9 us
    all_to_all x1, blocking collectives, body(): lax.all_to_all(copies, ('dp', 'expert'), split_axis=0, concat_axis=0, til...  30.7 us
    all_to_all x1, waiting for transfers between devices, body(): lax.all_to_all(partial_value.astype(jnp.bfloat16), ('dp', 'expert'), spli...  23.1 us
    gather x1, local copies, waits for them, and re-layouts, holder_block(): fetched = kv_pool[page_rows].reshape(blocks, token_span, 2 * width)  16.1 us
    pmax x1, blocking collectives, body(): peak_score = lax.pmax(highest, 'dp')  12.4 us
    psum x1, blocking collectives, body(): lax.psum((totals * factor).astype(jnp.bfloat16), 'dp').astype(jnp.float32)  10.5 us
    another operation x3, local copies, waits for them, and re-layouts, holder_block(): jnp.tile(query_heads, (1, 1, KVH))  9.71 us
    all_to_all x2, local copies, waits for them, and re-layouts, body(): lax.all_to_all(copies, ('dp', 'expert'), split_axis=0, concat_axis=0, til...  8.73 us
  transfers between devices with their start and end apart: 3, of which 3 were waited for; matrix products, arithmetic and copies ran while one was open for 1% of the time, Pallas kernels for 0%

commit v1 on v0

--- a/solution.py
+++ b/solution.py
@@ -12,6 +12,12 @@
 PPH = 16
 EPSILON = 1e-05
 LIMIT = 7.0
+
+
+def rest_ratios(dev_axis, view):
+    return jnp.concatenate(
+        lax.all_to_all(jnp.stack(lax.axis_size(dev_axis) * [view], 0), dev_axis, 0, 0), 0
+    )
 
 
 def rms_scale(values, gain):
@@ -94,7 +100,7 @@
     experts_count = lax.axis_size("expert")
     own_rows = queries.shape[0]
     tables, held_rows = (
-        lax.all_gather(page_table, "dp", axis=0, tiled=True),
+        rest_ratios("dp", page_table),
         lax.all_gather(held_tokens, "dp", axis=0, tiled=True),
     )
     group_queries = lax.all_gather(queries, "dp", axis=0, tiled=True)

time: 266 us -> 269 us (1.011)
  blocking collectives: 93 us -> 84 us
  starting transfers between devices: 9.51 us -> 16.1 us
  local copies, waits for them, and re-layouts: 51.1 us -> 54 us
    all_gather x1 -> x0, blocking collectives: 7.2 us -> none  [body(): lax.all_gather(page_table, 'dp', axis=0, tiled=True)]
    all_to_all x0 -> x1, starting transfers between devices: none -> 6.65 us  [rest_ratios(): lax.all_to_all(jnp.stack(lax.axis_size(dev_axis) * [view], 0), dev_axis,...]
  transfers between devices with their start and end apart: 3 -> 4, of which waited for: 3 -> 3; matrix products, arithmetic and copies ran while one was open for 1% -> 5% of each run, Pallas kernels for 0% -> 0%
where the time goes in v1:
time: 269 us; the launch traced here: 268 us
  blocking collectives  84 us (31%)
  waiting for transfers between devices  59.3 us (22%)
  local copies, waits for them, and re-layouts  54 us (20%)
  matrix products  33.2 us (12%)
  starting transfers between devices  16.1 us (6%)
  between operations  14.3 us (5%)
  other arithmetic  6.88 us (3%)
    psum x1, waiting for transfers between devices, body(): lax.psum(scale_heads(numerator, factor).astype(jnp.bfloat16), 'dp')  31.6 us
    all_to_all x1, blocking collectives, body(): lax.all_to_all(copies, ('dp', 'expert'), split_axis=0, concat_axis=0, til...  30.7 us
    all_to_all x1, waiting for transfers between devices, body(): lax.all_to_all(partial_value.astype(jnp.bfloat16), ('dp', 'expert'), spli...  23.1 us
    gather x1, local copies, waits for them, and re-layouts, holder_block(): fetched = kv_pool[page_rows].reshape(blocks, token_span, 2 * width)  16.1 us
    pmax x1, blocking collectives, body(): peak_score = lax.pmax(highest, 'dp')  12.4 us
    psum x1, blocking collectives, body(): lax.psum((totals * factor).astype(jnp.bfloat16), 'dp').astype(jnp.float32)  10.5 us
    another operation x3, local copies, waits for them, and re-layouts, holder_block(): jnp.tile(query_heads, (1, 1, KVH))  9.71 us
    all_to_all x2, local copies, waits for them, and re-layouts, body(): lax.all_to_all(copies, ('dp', 'expert'), split_axis=0, concat_axis=0, til...  8.73 us
  transfers between devices with their start and end apart: 4, of which 3 were waited for; matrix products, arithmetic and copies ran while one was open for 5% of the time, Pallas kernels for 0%

profile of v1, /device:TPU:1, one launch (start us, length us, event | category | flops | bytes accessed | tf_op | source)
XLA Modules:
  0.0 267.8 jit_solution(2783574315657916639)
XLA Ops:
  7.2 0.0 copy-start
  7.2 0.9 copy.34
  8.1 0.7 reshape.267
  8.8 6.6 %all-to-all-start = ((s32[4,1,512]{2,1,0:T(1,128)}), s32[4,1,512]{2,1,0:T(1,128)S(1)}, u32[]{:S(2)}, u32[]{:S(2)}) async-start(s32[4,1,512]{2,1,0:T(1,128)} %reshape.267), calls=%async_computation | async-start | bytes 16384 | tf_op jit(solution)/shard_map/all_to_all | solution.py:19
  15.4 0.8 copy.37
  16.2 0.7 fusion.68
  16.9 6.7 %all-gather = s32[4,8,4]{1,2,0:T(4,128)S(1)} all-gather(s32[1,8,4]{1,2,0:T(4,128)} %bitcast.67), channel_id=1, replica_groups=mesh['dp'=4,'expert'=32] {'dp'}, dimensions={0}, use_global_device_ids=true | all-gather | bytes 640 | tf_op jit(solution)/shard_map/all_gather | solution.py:104
  23.6 0.1 reshape.263
  23.7 0.1 iota_compare_fusion.2
  23.8 0.1 eq.93
  23.8 0.1 fusion.76
  23.9 0.1 reduce_window_sum.11
  24.0 0.2 select_reduce_fusion.1
  24.1 0.1 broadcast_compare_fusion
  24.2 7.9 %all_gather.10 = bf16[32,4096]{1,0:T(8,128)(2,1)S(1)} all-gather(bf16[8,4096]{1,0:T(8,128)(2,1)} %param.15), channel_id=1, replica_groups=mesh['dp'=4,'expert'=32] {'dp'}, dimensions={0}, use_global_device_ids=true | all-gather | bytes 327680 | tf_op jit(solution)/shard_map/all_gather | solution.py:106
  32.2 0.5 tile.14
  32.7 2.7 %tile.15 = bf16[32,64,8,64]{3,2,1,0:T(8,128)(2,1)} broadcast(bf16[32,64,64]{2,1,0:T(8,128)(2,1)S(1)} %tile.14), dimensions={0,1,3} | broadcast | bytes 2359296 | tf_op jit(solution)/shard_map/while/body/eval_jaxpr/tile | solution.py:53
  35.4 6.4 %tile.16 = bf16[32,64,512]{2,1,0:T(8,128)(2,1)} reshape(bf16[32,64,8,64]{3,2,1,0:T(8,128)(2,1)} %tile.15) | data formatting | bytes 4194304 | tf_op jit(solution)/shard_map/while/body/eval_jaxpr/tile | solution.py:53
  41.9 0.1 eq.97
  42.0 0.1 copy.38
  42.0 0.0 all-to-all-done
  42.1 0.5 broadcast.236
  42.6 0.7 reduce.3
  43.2 0.1 reshape.268
  43.4 0.1 reshape.254
  43.5 16.1 %gather_fusion = bf16[512,16,1024]{2,1,0:T(8,128)(2,1)} fusion(bf16[128,16,1024]{2,1,0:T(8,128)(2,1)} %param.16, s32[1024]{0:T(1024)S(1)} %pad_clamp_fusion), kind=kCustom, calls=%fused_computation | custom fusion | bytes 33556480 | tf_op jit(solution)/shard_map/while/body/eval_jaxpr/gather | solution.py:48
  59.5 8.0 %select_reduce_fusion = (f32[32,64]{1,0:T(8,128)S(1)}, f32[32,64,256]{2,1,0:T(8,128)}) fusion(pred[32,256]{1,0:T(8,128)(4,1)S(1)} %iota_compare_fusion.2, bf16[32,256,1024]{2,1,0:T(8,128)(2,1)} %bitcast.62, bf16[32,64,512]{2,1,0:T(8,128)(2,1)} %tile.16, pred[64,512]{1,0:T(8,128)(4,1)S(1)} %broadcast_compare_fusion), kind=kOutput, calls=%fused_computation.20 | convolution fusion | flops 539490304 | bytes 12632064 | tf_op jit(solution)/shard_map/while/body/eval_jaxpr/bhe,ble->bhl/dot_general | solution.py:55
  67.6 12.4 %pmax.7 = f32[32,64]{1,0:T(8,128)S(1)} all-reduce(f32[32,64]{1,0:T(8,128)S(1)} %get-tuple-element.28), channel_id=1, replica_groups=mesh['dp'=4,'expert'=32] {'dp'}, use_global_device_ids=true, to_apply=%region_1.2 | all-reduce | flops 2048 | bytes 16384 | tf_op jit(solution)/shard_map/pmax | solution.py:129
  80.0 2.5 fusion.17
  82.5 4.3 %fusion = f32[32,64,512]{2,1,0:T(8,128)S(1)} fusion(bf16[32,256,1024]{2,1,0:T(8,128)(2,1)} %bitcast.63, f32[32,64,256]{2,1,0:T(8,128)S(1)} %copy-done.1, f32[32,64]{1,0:T(8,128)S(1)} %get-tuple-element.28, pred[32,256]{1,0:T(8,128)(4,1)S(1)} %iota_compare_fusion.2), kind=kOutput, calls=%fused_computation.1 | convolution fusion | flops 538968064 | bytes 14696448 | tf_op jit(solution)/shard_map/while/body/eval_jaxpr/bhl,ble->bhe/dot_general | solution.py:62
  86.9 0.0 copy-start.7
  86.9 2.2 fusion.22
  89.1 1.2 convert_element_type.109
  90.3 0.0 all-reduce.2.cloned.1.call-update
  90.3 10.5 %psum.15 = bf16[32,64]{1,0:T(8,128)(2,1)S(1)} all-reduce(bf16[32,64]{1,0:T(8,128)(2,1)S(1)} %get-tuple-element.24), channel_id=1, replica_groups=mesh['dp'=4,'expert'=32] {'dp'}, use_global_device_ids=true, to_apply=%region_4.5 | all-reduce | flops 2048 | bytes 8192 | tf_op jit(solution)/shard_map/psum | solution.py:132
  100.9 0.3 broadcast_in_dim.108
  101.2 1.2 reshape.249
  102.4 31.6 %all-reduce.2.cloned.1.call-done = bf16[32,4096]{1,0:T(8,128)(2,1)} async-done(((bf16[32,4096]{1,0:T(8,128)(2,1)}), bf16[32,4096]{1,0:T(8,128)(2,1)}) %all-reduce.2.cloned.1.call-update) | async-done | bytes 262160 | tf_op jit(solution)/shard_map/psum | solution.py:133
  134.0 5.3 %fusion.40 = bf16[4,8,720]{2,1,0:T(8,128)(2,1)} fusion(bf16[4096,720]{0,1:T(8,128)(2,1)} %param.27, f32[32,4096]{1,0:T(8,128)} %reshape.249, bf16[32,4096]{1,0:T(8,128)(2,1)} %all-reduce.2.cloned.1.call-done), kind=kOutput, calls=%fused_computation.34 | convolution fusion | flops 189159936 | bytes 6730752 | tf_op jit(solution)/shard_map/dot_general | solution.py:140
  139.3 3.4 %all-to-all-start.1 = ((bf16[4,8,720]{2,1,0:T(8,128)(2,1)}), bf16[4,8,720]{2,1,0:T(8,128)(2,1)S(1)}, u32[]{:S(2)}, u32[]{:S(2)}) async-start(bf16[4,8,720]{2,1,0:T(8,128)(2,1)} %fusion.40), calls=%async_computation.1 | async-start | bytes 98304 | tf_op jit(solution)/shard_map/all_to_all | solution.py:143
  142.7 0.1 multiply_reduce_fusion
  142.8 4.6 %all-to-all-done.1 = bf16[4,8,720]{2,1,0:T(8,128)(2,1)S(1)} async-done(((bf16[4,8,720]{2,1,0:T(8,128)(2,1)}), bf16[4,8,720]{2,1,0:T(8,128)(2,1)S(1)}, u32[]{:S(2)}, u32[]{:S(2)}) %all-to-all-start.1) | async-done | bytes 46112 | tf_op jit(solution)/shard_map/all_to_all | solution.py:143
  147.5 0.1 reshape.250
  147.6 0.1 fusion.64
  147.8 0.3 convolution_convert_fusion.1
  148.1 1.2 broadcast_in_dim.109
  149.3 4.3 %all_to_all.44 = bf16[128,2,2880]{2,1,0:T(2,128)(2,1)} reshape(bf16[4,64,2880]{2,1,0:T(8,128)(2,1)} %broadcast_in_dim.109) | data formatting | bytes 2949120 | tf_op jit(solution)/shard_map/all_to_all | solution.py:171
  153.6 30.7 %all_to_all.58 = bf16[128,2,2880]{2,1,0:T(2,128)(2,1)} all-to-all(bf16[128,2,2880]{2,1,0:T(2,128)(2,1)} %all_to_all.44), channel_id=1, replica_groups=mesh['dp'=4,'expert'=32] {'dp','expert'}, dimensions={0} | all-to-all | bytes 2949120 | tf_op jit(solution)/shard_map/all_to_all | solution.py:171
  184.3 4.4 %all_to_all.46 = bf16[256,2880]{1,0:T(8,128)(2,1)} reshape(bf16[128,2,2880]{2,1,0:T(2,128)(2,1)} %all_to_all.58) | data formatting | bytes 2949120 | tf_op jit(solution)/shard_map/all_to_all | solution.py:171
  188.7 3.0 %fusion.25 = f32[256,384]{1,0:T(8,128)S(1)} fusion(bf16[256,2880]{1,0:T(8,128)(2,1)} %all_to_all.46, bf16[1,2880,384]{2,1,0:T(8,128)(2,1)} %param.24), kind=kOutput, calls=%fused_computation.28 | convolution fusion | flops 566329344 | bytes 4079616 | tf_op jit(solution)/shard_map/dot_general | solution.py:74
  191.8 5.1 %convolution_convert_fusion = bf16[256,2880]{0,1:T(8,128)(2,1)} fusion(bf16[1,384,2880]{1,2,0:T(8,128)(2,1)S(1)} %copy-done, bf16[256,2880]{1,0:T(8,128)(2,1)} %all_to_all.46, bf16[1,2880,384]{2,1,0:T(8,128)(2,1)} %param.25, f32[256,384]{1,0:T(8,128)S(1)} %fusion.25), kind=kOutput, calls=%fused_computation.7 | convolution fusion | flops 1134084096 | bytes 7766016 | tf_op jit(solution)/shard_map/dot_general | solution.py:79
  196.8 2.6 copy.39
  199.4 4.3 %all_to_all.47 = bf16[128,2,2880]{2,1,0:T(2,128)(2,1)} reshape(bf16[256,2880]{1,0:T(8,128)(2,1)} %copy.39) | data formatting | bytes 2949120 | tf_op jit(solution)/shard_map/all_to_all | solution.py:173
  203.7 6.1 %all-to-all-start.3 = ((bf16[128,2,2880]{2,1,0:T(2,128)(2,1)}), bf16[128,2,2880]{2,1,0:T(2,128)(2,1)}, u32[]{:S(2)}, u32[]{:S(2)}) async-start(bf16[128,2,2880]{2,1,0:T(2,128)(2,1)} %all_to_all.47), calls=%async_computation.3 | async-start | bytes 3014656 | tf_op jit(solution)/shard_map/all_to_all | solution.py:173
  209.8 23.1 %all-to-all-done.3 = bf16[128,2,2880]{2,1,0:T(2,128)(2,1)} async-done(((bf16[128,2,2880]{2,1,0:T(2,128)(2,1)}), bf16[128,2,2880]{2,1,0:T(2,128)(2,1)}, u32[]{:S(2)}, u32[]{:S(2)}) %all-to-all-start.3) | async-done | bytes 1474592 | tf_op jit(solution)/shard_map/all_to_all | solution.py:173
  233.0 4.5 %reshape.251 = f32[4,64,2880]{2,1,0:T(8,128)} reshape(bf16[128,2,2880]{2,1,0:T(2,128)(2,1)} %all-to-all-done.3) | data formatting | bytes 4423680 | tf_op jit(solution)/shard_map/convert_element_type | solution.py:179
  237.5 2.1 reduce_sum.69
  239.6 0.6 fusion.61
  240.2 0.0 copy-start.2
  240.2 0.1 fusion.63
  240.3 8.4 %all_gather.11 = bf16[32,2880]{1,0:T(8,128)(2,1)S(1)} all-gather(bf16[8,2880]{1,0:T(8,128)(2,1)S(1)} %fusion.63), channel_id=1, replica_groups=mesh['dp'=4,'expert'=32] {'dp'}, dimensions={0}, use_global_device_ids=true | all-gather | bytes 230400 | tf_op jit(solution)/shard_map/all_gather | solution.py:187
  248.7 4.3 %fusion.7 = bf16[4,8,1280]{2,1,0:T(8,128)(2,1)S(1)} fusion(bf16[32,2880]{1,0:T(8,128)(2,1)S(1)} %all_gather.11, bf16[2880,1280]{1,0:T(8,128)(2,1)} %param.29), kind=kOutput, calls=%fused_computation.12 | convolution fusion | flops 235970560 | bytes 7639040 | tf_op jit(solution)/shard_map/dot_general | solution.py:186
  253.0 7.3 %all_to_all.59 = bf16[4,8,1280]{2,1,0:T(8,128)(2,1)S(1)} all-to-all(bf16[4,8,1280]{2,1,0:T(8,128)(2,1)S(1)} %fusion.7), channel_id=1, replica_groups=mesh['dp'=4,'expert'=32] {'dp'}, dimensions={0} | all-to-all | bytes 163840 | tf_op jit(solution)/shard_map/all_to_all | solution.py:191
  260.3 0.6 copy.50
  (34 shorter events, 0.2 us)
Async XLA Ops:
  7.2 184.6 %copy-start = (bf16[1,384,2880]{1,2,0:T(8,128)(2,1)S(1)}, bf16[1,384,2880]{1,2,0:T(8,128)(2,1)}, u32[]{:S(2)}) copy-start(bf16[1,384,2880]{1,2,0:T(8,128)(2,1)} %param.26) | copy-start | bytes 6635524
  8.8 33.3 %all-to-all-start = ((s32[4,1,512]{2,1,0:T(1,128)}), s32[4,1,512]{2,1,0:T(1,128)S(1)}, u32[]{:S(2)}, u32[]{:S(2)}) async-start(s32[4,1,512]{2,1,0:T(1,128)} %reshape.267), calls=%async_computation | async-start | bytes 16384 | tf_op jit(solution)/shard_map/all_to_all | solution.py:19
  15.4 118.6 %all-reduce.2.cloned.1.call-start = ((), (), s32[]{:S(2)}) async-start(), calls=%async_computation.5 | async-start | bytes 524288 | tf_op jit(solution)/shard_map/psum | solution.py:133
  80.0 2.5 copy-start.1
  86.9 14.0 %copy-start.7 = (f32[64]{0:T(128)S(1)}, f32[64]{0:T(128)}, u32[]{:S(2)}) copy-start(f32[64]{0:T(128)} %param.19) | copy-start | bytes 772
  102.4 45.3 %copy-start.3 = (bf16[8,2880]{1,0:T(8,128)(2,1)S(1)}, bf16[8,2880]{1,0:T(8,128)(2,1)}, u32[]{:S(2)}) copy-start(bf16[8,2880]{1,0:T(8,128)(2,1)} %param.20) | copy-start | bytes 138244
  102.4 45.4 %copy-start.5 = (f32[2880]{0:T(1024)S(1)}, f32[2880]{0:T(1024)}, u32[]{:S(2)}) copy-start(f32[2880]{0:T(1024)} %param.23) | copy-start | bytes 34564
  139.3 8.1 %all-to-all-start.1 = ((bf16[4,8,720]{2,1,0:T(8,128)(2,1)}), bf16[4,8,720]{2,1,0:T(8,128)(2,1)S(1)}, u32[]{:S(2)}, u32[]{:S(2)}) async-start(bf16[4,8,720]{2,1,0:T(8,128)(2,1)} %fusion.40), calls=%async_computation.1 | async-start | bytes 98304 | tf_op jit(solution)/shard_map/all_to_all | solution.py:143
  203.7 6.1 %copy-start.6 = (f32[8,4]{0,1:T(4,128)S(1)}, f32[8,4]{0,1:T(4,128)}, u32[]{:S(2)}) copy-start(f32[8,4]{0,1:T(4,128)} %param.22) | copy-start | bytes 388
  203.7 29.3 %all-to-all-start.3 = ((bf16[128,2,2880]{2,1,0:T(2,128)(2,1)}), bf16[128,2,2880]{2,1,0:T(2,128)(2,1)}, u32[]{:S(2)}, u32[]{:S(2)}) async-start(bf16[128,2,2880]{2,1,0:T(2,128)(2,1)} %all_to_all.47), calls=%async_computation.3 | async-start | bytes 3014656 | tf_op jit(solution)/shard_map/all_to_all | solution.py:173
  237.5 2.7 %copy-start.4 = (f32[2880]{0:T(1024)S(1)}, f32[2880]{0:T(1024)}, u32[]{:S(2)}) copy-start(f32[2880]{0:T(1024)} %param.28) | copy-start | bytes 34564
  240.2 12.8 %copy-start.2 = (bf16[8,2880]{1,0:T(8,128)(2,1)}, bf16[8,2880]{1,0:T(8,128)(2,1)S(1)}, u32[]{:S(2)}) copy-start(bf16[8,2880]{1,0:T(8,128)(2,1)S(1)} %get-tuple-element.44) | copy-start | bytes 138244
Sparse Core Ops, SparseCore 0:
  90.4 43.4 all-reduce.1
